TPU v7x, 32 devices: a whole 2x2x4 slice. The times are simulated.
32 devices in a mesh: pages: 16 (over z, x, core), tok: 2 (over y).
Axes of the slice: x: 2, y: 2, z: 4, core: 2. Of those that a mesh axis runs over, the one named last changes fastest.
Arguments:
- queries: bfloat16 [32, 32, 128], P('pages'), may hold values from -50 to 50
- pages: bfloat16 [16, 1024, 128], P('pages', 'tok'), may hold values from -10 to 10
- pad_counts: int32 [16], P('pages'), may hold values from 0 to 511
- labels: int32 [32, 16], P(None, 'pages'), may hold values 0 or 1
Outputs:
- query_grad: float32 [32, 32, 128], P('pages')
- page_grad: float32 [16, 1024, 128], P('pages', 'tok')
- page_loss: float32 [16], P('pages')
All inputs are finite; a program needn't handle non-finite values. No bound on the sum of `labels` on one device may be relied on, other than what follows from the above.
Results may differ from a plain program's by a relative error of at most 0.0025.
Values may be sent and summed in bfloat16 or wider, within the bound.
No kernel may reach another device: no remote copies, remote signals or barrier semaphores. Data moves between devices by JAX's collectives and lax.ppermute only.
A program may use at most 64 MiB of HBM per device.

v0:
```python
import math
import jax
import jax.numpy as jnp
from jax import lax
from jax.sharding import PartitionSpec as P

LP = 1024
MASKED = -1000000000.0
LOGIT_SPAN = 8.0
CENTRE_SHIFT = 0.5
FILL_SHARE = 0.75


def combined_all(value, axis, combine):
    everything = lax.all_gather(value, axis)
    first = everything[0]

    def lap(k, so_far):
        return combine(so_far, everything[k])

    return lax.fori_loop(1, lax.axis_size(axis), lap, first)


def combine_smooth(former, latter):
    highest = jnp.maximum(former, latter)
    return highest + jnp.log(jnp.exp(former - highest) + jnp.exp(latter - highest))


def on_device(queries, pages, pad_counts, labels):
    query_count, query_len, feature_width = queries.shape
    local_pages, local_tokens, _ = pages.shape
    score_scale = feature_width ** (-0.5)
    token_offset = lax.axis_index("tok") * local_tokens
    positions = token_offset + jnp.arange(local_tokens, dtype=jnp.int32)
    usable = positions[None, :] < (LP - pad_counts)[:, None]
    gathered = lax.all_gather(queries, "pages", axis=0, tiled=True)
    query_total = gathered.shape[0]
    row_count = query_total * query_len
    query_rows = gathered.reshape(row_count, feature_width)
    block_rows = math.gcd(row_count, 512)
    block_count = row_count // block_rows

    def scores_for(query_block, page_no):
        raw = (
            lax.dot_general(
                query_block,
                pages[page_no],
                (((1,), (1,)), ((), ())),
                preferred_element_type=jnp.float32,
            )
            * score_scale
        )
        return jnp.where(usable[page_no][None, :], raw, MASKED)

    def forward_block(block_index, running):
        offset = block_index * block_rows
        query_block = lax.dynamic_slice_in_dim(query_rows, offset, block_rows, 0)
        scores = scores_for(query_block, 0)
        highest = jnp.max(scores, axis=1)
        columns = [highest + jnp.log(jnp.sum(jnp.exp(scores - highest[:, None]), axis=1))]
        partial_value = jnp.stack(columns, axis=1)
        return lax.dynamic_update_slice_in_dim(running, partial_value, offset, 0)

    buffered = lax.fori_loop(
        0, block_count, forward_block, jnp.zeros((row_count, local_pages), jnp.float32)
    )
    smooth = combined_all(buffered, "tok", combine_smooth)
    similarity = smooth.reshape(query_total, query_len, local_pages).sum(axis=1)
    label_sign = 2.0 * labels.astype(jnp.float32) - 1.0
    logit_gain = LOGIT_SPAN / query_len
    centre = query_len * (CENTRE_SHIFT + math.log(FILL_SHARE * LP))
    logits = logit_gain * (similarity - centre)
    page_loss = jnp.sum(jax.nn.softplus(-label_sign * logits), axis=0)
    slope = logit_gain * (-label_sign * jax.nn.sigmoid(-label_sign * logits))
    row_slope = jnp.repeat(slope, query_len, axis=0)

    def backward_block(block_index, running):
        query_terms, page_terms = running
        offset = block_index * block_rows
        query_block = lax.dynamic_slice_in_dim(query_rows, offset, block_rows, 0)
        smooth_block = lax.dynamic_slice_in_dim(smooth, offset, block_rows, 0)
        slope_block = lax.dynamic_slice_in_dim(row_slope, offset, block_rows, 0)
        scores = scores_for(query_block, 0)
        weights = jnp.where(usable[0][None, :], jnp.exp(scores - smooth_block[:, 0][:, None]), 0.0)
        scaled = (weights * slope_block[:, 0][:, None]).astype(jnp.bfloat16)
        summed = jnp.dot(scaled, pages[0], preferred_element_type=jnp.float32)
        gradients = [
            lax.dot_general(
                scaled, query_block, (((0,), (0,)), ((), ())), preferred_element_type=jnp.float32
            )
        ]
        page_terms = page_terms + jnp.stack(gradients, axis=0)
        query_terms = lax.dynamic_update_slice_in_dim(query_terms, summed * score_scale, offset, 0)
        return (query_terms, page_terms)

    start_terms = (
        jnp.zeros((row_count, feature_width), jnp.float32),
        jnp.zeros((local_pages, local_tokens, feature_width), jnp.float32),
    )
    query_terms, page_terms = lax.fori_loop(0, block_count, backward_block, start_terms)
    page_grad = page_terms * score_scale
    owned = lax.psum_scatter(query_terms, "pages", scatter_dimension=0, tiled=True)
    owned = lax.psum(owned, "tok")
    query_grad = owned.reshape(query_count, query_len, feature_width)
    return (query_grad, page_grad, page_loss)


def solution(mesh):
    return jax.shard_map(
        on_device,
        mesh=mesh,
        in_specs=(P("pages", None, None), P("pages", "tok", None), P("pages"), P(None, "pages")),
        out_specs=(P("pages", None, None), P("pages", "tok", None), P("pages")),
        check_vma=False,
    )
```

profile of v0, /device:TPU:0, one launch (start us, length us, event | category | flops | bytes accessed | tf_op | source)
XLA Modules:
  0.0 112.6 jit_solution(9280587860546555923)
XLA Ops:
  7.2 0.0 reduce-scatter.2.cloned.1.call-start
  7.9 0.0 copy-start
  7.9 24.2 %all_gather.9 = bf16[32,32,128]{2,1,0:T(8,128)(2,1)S(1)} all-gather(bf16[2,32,128]{2,1,0:T(8,128)(2,1)} %param.8), channel_id=1, replica_groups=mesh['pages'=16,'tok'=2] {'pages'}, dimensions={0}, use_global_device_ids=true | all-gather | bytes 278528 | tf_op jit(solution)/shard_map/all_gather | solution.py:36
  32.1 0.0 copy-done
  32.1 1.2 %while.35 = (s32[]{:T(128)}, f32[1024,1]{0,1:T(1,128)S(1)}, bf16[1024,128]{1,0:T(8,128)(2,1)S(1)}, bf16[1,512,128]{2,1,0:T(8,128)(2,1)S(1)}, s32[]{:T(128)}, /*i...) while((s32[]{:T(128)}, f32[1024,1]{0,1:T(1,128)S(1)}, ...), condition=%wide.region_3.4_spmd.clone, body=%wide.region_0.3_spmd.clone.sunk | while | flops 68420104 | bytes 2376867 | solution.py:64
  32.1 0.3 fusion.38
  32.4 0.2 exponential_reduce_fusion.2
  32.7 0.3 fusion.38
  33.0 0.2 exponential_reduce_fusion.2
  33.2 4.4 %all-gather = f32[2048,1]{0,1:T(1,128)S(1)} all-gather(f32[1024,1]{0,1:T(1,128)S(1)} %get-tuple-element.249), channel_id=2, replica_groups=mesh['pages'=16,'tok'=2] {'tok'}, dimensions={0}, use_global_device_ids=true | all-gather | bytes 12288 | tf_op jit(solution)/shard_map/all_gather | solution.py:15
  37.6 0.1 squeeze.28
  37.7 0.1 squeeze.29
  37.8 0.0 copy-start.2
  37.8 0.1 add_reduce_fusion
  37.9 0.5 copy-done.2
  38.4 0.6 fusion.24
  39.1 0.1 broadcast_in_dim.84
  39.2 0.1 broadcast_in_dim.85
  39.3 2.4 %while.36 = (s32[]{:T(128)}, f32[1024,128]{1,0:T(8,128)S(1)}, f32[1,512,128]{2,1,0:T(8,128)S(1)}, bf16[1024,128]{1,0:T(8,128)(2,1)S(1)}, bf16[1,512,128]{2,1,0:T...) while((s32[]{:T(128)}, f32[1024,128]{1,0:T(8,128)S(1)}, ...), condition=%wide.region_6.7_spmd.clone, body=%wide.region_5.6_spmd.clone.sunk | while | flops 203097088 | bytes 2897109 | solution.py:100
  39.4 0.4 fusion.45
  39.8 0.4 fusion.47
  40.2 0.3 fusion.46
  40.5 0.4 fusion.45
  41.0 0.4 fusion.47
  41.4 0.3 fusion.46
  41.7 0.0 copy-start.1
  41.7 0.8 copy-done.1
  42.5 0.0 reduce-scatter.2.cloned.1.call-update
  42.5 0.7 broadcast_multiply_fusion
  43.2 52.9 %reduce-scatter.2.cloned.1.call-done = f32[64,128]{1,0:T(8,128)} async-done(((f32[1024,128]{1,0:T(8,128)}), f32[64,128]{1,0:T(8,128)}) %reduce-scatter.2.cloned.1.call-update) | async-done | bytes 32784 | tf_op jit(solution)/shard_map/reduce_scatter | solution.py:102
  96.2 9.6 %psum.7 = f32[2,32,128]{2,1,0:T(8,128)} all-reduce(f32[2,32,128]{2,1,0:T(8,128)} %bitcast.50), channel_id=1, replica_groups=mesh['pages'=16,'tok'=2] {'tok'}, use_global_device_ids=true, to_apply=%region_8.9 | all-reduce | flops 8192 | bytes 65536 | tf_op jit(solution)/shard_map/psum | solution.py:103
  (15 shorter events, 0.3 us)
Async XLA Ops:
  7.2 89.0 %reduce-scatter.2.cloned.1.call-start = ((), (), s32[]{:S(2)}) async-start(), calls=%async_computation.1 | async-start | bytes 557056 | tf_op jit(solution)/shard_map/reduce_scatter | solution.py:102
  7.9 24.2 %copy-start = (bf16[1,512,128]{2,1,0:T(8,128)(2,1)S(1)}, bf16[1,512,128]{2,1,0:T(8,128)(2,1)}, u32[]{:S(2)}) copy-start(bf16[1,512,128]{2,1,0:T(8,128)(2,1)} %param.9) | copy-start | bytes 393220
  37.8 0.7 copy-start.2
  41.7 0.8 copy-start.1
Sparse Core Ops, SparseCore 0:
  42.6 53.4 reduce-scatter.1
where the time goes:
time: 113 us
  waiting for transfers between devices  52.9 us (47%)
  blocking collectives  38.1 us (34%)
  between operations  14.7 us (13%)
  matrix products  2.87 us (3%)
  other arithmetic  2.05 us (2%)
  local copies, waits for them, and re-layouts  1.7 us (2%)
    reduce_scatter x1, waiting for transfers between devices, on_device(): lax.psum_scatter(query_terms, 'pages', scatter_dimension=0, tiled=True)  52.9 us
    all_gather x1, blocking collectives, on_device(): gathered = lax.all_gather(queries, 'pages', axis=0, tiled=True)  24.2 us
    psum x1, blocking collectives, on_device(): owned = lax.psum(owned, 'tok')  9.55 us
    all_gather x1, blocking collectives, combined_all(): everything = lax.all_gather(value, axis)  4.36 us
  transfers between devices with their start and end apart: 1, of which 1 were waited for; matrix products, arithmetic and copies ran while one was open for 1% of the time, Pallas kernels for 0%

commit v1 on v0

--- a/solution.py
+++ b/solution.py
@@ -33,7 +33,16 @@
     token_offset = lax.axis_index("tok") * local_tokens
     positions = token_offset + jnp.arange(local_tokens, dtype=jnp.int32)
     usable = positions[None, :] < (LP - pad_counts)[:, None]
-    gathered = lax.all_gather(queries, "pages", axis=0, tiled=True)
+    ways = lax.axis_size("pages")
+    up = [(d, (d + 1) % ways) for d in range(ways)]
+    down = [(d, (d - 1) % ways) for d in range(ways)]
+    earlier, later = ([queries], [queries])
+    for _ in range(ways // 2):
+        earlier.append(lax.ppermute(earlier[-1], "pages", up))
+    for _ in range((ways - 1) // 2):
+        later.append(lax.ppermute(later[-1], "pages", down))
+    line = jnp.concatenate([*earlier[::-1], *later[1:]], axis=0)
+    gathered = jnp.roll(line, (lax.axis_index("pages") - ways // 2) * queries.shape[0], axis=0)
     query_total = gathered.shape[0]
     row_count = query_total * query_len
     query_rows = gathered.reshape(row_count, feature_width)

time: 113 us -> 141 us (1.25)
  starting transfers between devices: 0.04 us -> 31.6 us
  blocking collectives: 38.1 us -> 13.9 us
  waiting for transfers between devices: 52.9 us -> 71.9 us
  local copies, waits for them, and re-layouts: 1.7 us -> 3.56 us
    ppermute x0 -> x15, starting transfers between devices: none -> 31.6 us  [the longest x7 31 us: on_device(): later.append(lax.ppermute(later[-1], 'pages', down))]
    all_gather x1 -> x0, blocking collectives: 24.2 us -> none  [on_device(): gathered = lax.all_gather(queries, 'pages', axis=0, tiled=True)]
    ppermute x0 -> x15, waiting for transfers between devices: none -> 15.9 us  [the longest x8 14.7 us: on_device(): earlier.append(lax.ppermute(earlier[-1], 'pages', up))]
    reduce_scatter x1, waiting for transfers between devices: 52.9 us -> 56 us  [on_device(): lax.psum_scatter(query_terms, 'pages', scatter_dimension=0, tiled=True)]
    unnamed x6 -> x39, local copies, waits for them, and re-layouts: 1.31 us -> 3.14 us
  transfers between devices with their start and end apart: 1 -> 16, of which waited for: 1 -> 14; matrix products, arithmetic and copies ran while one was open for 1% -> 1% of each run, Pallas kernels for 0% -> 0%
where the time goes in v1:
time: 141 us
  waiting for transfers between devices  71.9 us (51%)
  starting transfers between devices  31.6 us (22%)
  between operations  14.9 us (11%)
  blocking collectives  13.9 us (10%)
  local copies, waits for them, and re-layouts  3.56 us (3%)
  matrix products  2.87 us (2%)
  other arithmetic  2.05 us (1%)
    reduce_scatter x1, waiting for transfers between devices, on_device(): lax.psum_scatter(query_terms, 'pages', scatter_dimension=0, tiled=True)  56 us
    ppermute x7, starting transfers between devices, on_device(): later.append(lax.ppermute(later[-1], 'pages', down))  31 us
    ppermute x8, waiting for transfers between devices, on_device(): earlier.append(lax.ppermute(earlier[-1], 'pages', up))  14.7 us
    psum x1, blocking collectives, on_device(): owned = lax.psum(owned, 'tok')  9.57 us
    all_gather x1, blocking collectives, combined_all(): everything = lax.all_gather(value, axis)  4.36 us
    unnamed x39, local copies, waits for them, and re-layouts  3.14 us
  transfers between devices with their start and end apart: 16, of which 14 were waited for; matrix products, arithmetic and copies ran while one was open for 1% of the time, Pallas kernels for 0%

profile of v1, /device:TPU:0, one launch (start us, length us, event | category | flops | bytes accessed | tf_op | source)
XLA Modules:
  0.0 140.9 jit_solution(4774161091867445454)
XLA Ops:
  7.2 0.0 reduce-scatter.2.cloned.1.call-start
  7.2 0.5 collective-permute-start
  7.8 6.6 %collective-permute-done = bf16[2,32,128]{2,1,0:T(8,128)(2,1)S(1)} collective-permute-done((bf16[2,32,128]{2,1,0:T(8,128)(2,1)}, bf16[2,32,128]{2,1,0:T(8,128)(2,1)S(1)}, u32[]{:S(2)}, u32[]{:S(2)}) %collective-permute-start) | collective-permute-done | bytes 16416 | tf_op jit(solution)/shard_map/ppermute | solution.py:41
  14.3 4.4 %collective-permute-start.8 = (bf16[2,32,128]{2,1,0:T(8,128)(2,1)}, bf16[2,32,128]{2,1,0:T(8,128)(2,1)S(1)}, u32[]{:S(2)}, u32[]{:S(2)}) collective-permute-start(bf16[2,32,128]{2,1,0:T(8,128)(2,1)} %param.8), channel_id=1, source_target_pairs={{0,30},{2,0},{4,2},{6,4},{8,6},{10,8},{12,10},{14,12},{16,14},{18,... | collective-permute-start | bytes 49160 | tf_op jit(solution)/shard_map/ppermute | solution.py:43
  18.8 1.4 %collective-permute-done.1 = bf16[2,32,128]{2,1,0:T(8,128)(2,1)S(1)} collective-permute-done((bf16[2,32,128]{2,1,0:T(8,128)(2,1)S(1)}, bf16[2,32,128]{2,1,0:T(8,128)(2,1)S(1)}, u32[]{:S(2)}, u32[]{:S(2)}) %collective-permute-start.1) | collective-permute-done | bytes 16416 | tf_op jit(solution)/shard_map/ppermute | solution.py:41
  20.2 0.2 collective-permute-done.8
  20.4 4.4 %collective-permute-start.9 = (bf16[2,32,128]{2,1,0:T(8,128)(2,1)S(1)}, bf16[2,32,128]{2,1,0:T(8,128)(2,1)S(1)}, u32[]{:S(2)}, u32[]{:S(2)}) collective-permute-start(bf16[2,32,128]{2,1,0:T(8,128)(2,1)S(1)} %collective-permute-done.8), channel_id=1, source_target_pairs={{0,30},{2,0},{4,2},{6,4},{8,6},{10,8},{12,10},{14,12},{16,14},{18,... | collective-permute-start | bytes 49160 | tf_op jit(solution)/shard_map/ppermute | solution.py:43
  24.9 1.2 collective-permute-done.2
  26.1 0.2 collective-permute-done.9
  26.3 4.4 %collective-permute-start.10 = (bf16[2,32,128]{2,1,0:T(8,128)(2,1)S(1)}, bf16[2,32,128]{2,1,0:T(8,128)(2,1)S(1)}, u32[]{:S(2)}, u32[]{:S(2)}) collective-permute-start(bf16[2,32,128]{2,1,0:T(8,128)(2,1)S(1)} %collective-permute-done.9), channel_id=1, source_target_pairs={{0,30},{2,0},{4,2},{6,4},{8,6},{10,8},{12,10},{14,12},{16,14},{18,... | collective-permute-start | bytes 49160 | tf_op jit(solution)/shard_map/ppermute | solution.py:43
  30.7 1.2 collective-permute-done.3
  31.9 0.2 collective-permute-done.10
  32.2 4.4 %collective-permute-start.11 = (bf16[2,32,128]{2,1,0:T(8,128)(2,1)S(1)}, bf16[2,32,128]{2,1,0:T(8,128)(2,1)S(1)}, u32[]{:S(2)}, u32[]{:S(2)}) collective-permute-start(bf16[2,32,128]{2,1,0:T(8,128)(2,1)S(1)} %collective-permute-done.10), channel_id=1, source_target_pairs={{0,30},{2,0},{4,2},{6,4},{8,6},{10,8},{12,10},{14,12},{16,14},{18,... | collective-permute-start | bytes 49160 | tf_op jit(solution)/shard_map/ppermute | solution.py:43
  36.6 1.2 collective-permute-done.4
  37.8 0.2 collective-permute-done.11
  38.0 4.4 %collective-permute-start.12 = (bf16[2,32,128]{2,1,0:T(8,128)(2,1)S(1)}, bf16[2,32,128]{2,1,0:T(8,128)(2,1)S(1)}, u32[]{:S(2)}, u32[]{:S(2)}) collective-permute-start(bf16[2,32,128]{2,1,0:T(8,128)(2,1)S(1)} %collective-permute-done.11), channel_id=1, source_target_pairs={{0,30},{2,0},{4,2},{6,4},{8,6},{10,8},{12,10},{14,12},{16,14},{18,... | collective-permute-start | bytes 49160 | tf_op jit(solution)/shard_map/ppermute | solution.py:43
  42.4 1.2 collective-permute-done.5
  43.7 0.2 collective-permute-done.12
  43.9 4.4 %collective-permute-start.13 = (bf16[2,32,128]{2,1,0:T(8,128)(2,1)S(1)}, bf16[2,32,128]{2,1,0:T(8,128)(2,1)S(1)}, u32[]{:S(2)}, u32[]{:S(2)}) collective-permute-start(bf16[2,32,128]{2,1,0:T(8,128)(2,1)S(1)} %collective-permute-done.12), channel_id=1, source_target_pairs={{0,30},{2,0},{4,2},{6,4},{8,6},{10,8},{12,10},{14,12},{16,14},{18,... | collective-permute-start | bytes 49160 | tf_op jit(solution)/shard_map/ppermute | solution.py:43
  48.3 1.2 collective-permute-done.6
  50.2 4.5 %collective-permute-start.14 = (bf16[2,32,128]{2,1,0:T(8,128)(2,1)S(1)}, bf16[2,32,128]{2,1,0:T(8,128)(2,1)S(1)}, u32[]{:S(2)}, u32[]{:S(2)}) collective-permute-start(bf16[2,32,128]{2,1,0:T(8,128)(2,1)S(1)} %collective-permute-done.13), channel_id=1, source_target_pairs={{0,30},{2,0},{4,2},{6,4},{8,6},{10,8},{12,10},{14,12},{16,14},{18,... | collective-permute-start | bytes 49160 | tf_op jit(solution)/shard_map/ppermute | solution.py:43
  54.7 0.7 collective-permute-done.7
  55.5 0.7 copy-done.2
  56.5 0.8 copy-done
  57.4 1.2 while.35
  57.4 0.3 fusion.38
  57.7 0.2 exponential_reduce_fusion.2
  58.0 0.3 fusion.38
  58.3 0.2 exponential_reduce_fusion.2
  58.6 4.4 %all-gather = f32[2048,1]{0,1:T(1,128)S(1)} all-gather(f32[1024,1]{0,1:T(1,128)S(1)} %get-tuple-element.249), channel_id=2, replica_groups=mesh['pages'=16,'tok'=2] {'tok'}, dimensions={0}, use_global_device_ids=true | all-gather | bytes 12288 | tf_op jit(solution)/shard_map/all_gather | solution.py:15
  63.0 0.1 squeeze.28
  63.0 0.1 squeeze.29
  63.1 0.1 add_reduce_fusion
  63.2 0.5 copy-done.3
  63.8 0.6 fusion.24
  64.4 0.1 broadcast_in_dim.84
  64.5 0.1 broadcast_in_dim.85
  64.6 2.4 %while.36 = (s32[]{:T(128)}, f32[1024,128]{1,0:T(8,128)S(1)}, f32[1,512,128]{2,1,0:T(8,128)S(1)}, bf16[1024,128]{1,0:T(8,128)(2,1)S(1)}, bf16[1,512,128]{2,1,0:T...) while((s32[]{:T(128)}, f32[1024,128]{1,0:T(8,128)S(1)}, ...), condition=%wide.region_6.7_spmd.clone, body=%wide.region_5.6_spmd.clone.sunk | while | flops 203097088 | bytes 2897109 | solution.py:109
  64.7 0.4 fusion.45
  65.1 0.4 fusion.47
  65.5 0.3 fusion.46
  65.9 0.4 fusion.45
  66.3 0.4 fusion.47
  66.7 0.3 fusion.46
  67.0 0.8 copy-done.1
  67.8 0.7 broadcast_multiply_fusion
  68.5 56.0 %reduce-scatter.2.cloned.1.call-done = f32[64,128]{1,0:T(8,128)} async-done(((f32[1024,128]{1,0:T(8,128)}), f32[64,128]{1,0:T(8,128)}) %reduce-scatter.2.cloned.1.call-update) | async-done | bytes 32784 | tf_op jit(solution)/shard_map/reduce_scatter | solution.py:111
  124.5 9.6 %psum.7 = f32[2,32,128]{2,1,0:T(8,128)} all-reduce(f32[2,32,128]{2,1,0:T(8,128)} %bitcast.50), channel_id=1, replica_groups=mesh['pages'=16,'tok'=2] {'tok'}, use_global_device_ids=true, to_apply=%region_8.9 | all-reduce | flops 8192 | bytes 65536 | tf_op jit(solution)/shard_map/psum | solution.py:112
  (62 shorter events, 0.6 us)
Async XLA Ops:
  7.2 117.4 %reduce-scatter.2.cloned.1.call-start = ((), (), s32[]{:S(2)}) async-start(), calls=%async_computation.1 | async-start | bytes 557056 | tf_op jit(solution)/shard_map/reduce_scatter | solution.py:111
  7.2 7.1 %collective-permute-start = (bf16[2,32,128]{2,1,0:T(8,128)(2,1)}, bf16[2,32,128]{2,1,0:T(8,128)(2,1)S(1)}, u32[]{:S(2)}, u32[]{:S(2)}) collective-permute-start(bf16[2,32,128]{2,1,0:T(8,128)(2,1)} %param.8), channel_id=1, source_target_pairs={{0,2},{2,4},{4,6},{6,8},{8,10},{10,12},{12,14},{14,16},{16,18},{18... | collective-permute-start | bytes 49160 | tf_op jit(solution)/shard_map/ppermute | solution.py:41
  14.3 5.9 %collective-permute-start.1 = (bf16[2,32,128]{2,1,0:T(8,128)(2,1)S(1)}, bf16[2,32,128]{2,1,0:T(8,128)(2,1)S(1)}, u32[]{:S(2)}, u32[]{:S(2)}) collective-permute-start(bf16[2,32,128]{2,1,0:T(8,128)(2,1)S(1)} %collective-permute-done), channel_id=1, source_target_pairs={{0,2},{2,4},{4,6},{6,8},{8,10},{10,12},{12,14},{14,16},{16,18},{18... | collective-permute-start | bytes 49160 | tf_op jit(solution)/shard_map/ppermute | solution.py:41
  14.3 6.1 %collective-permute-start.8 = (bf16[2,32,128]{2,1,0:T(8,128)(2,1)}, bf16[2,32,128]{2,1,0:T(8,128)(2,1)S(1)}, u32[]{:S(2)}, u32[]{:S(2)}) collective-permute-start(bf16[2,32,128]{2,1,0:T(8,128)(2,1)} %param.8), channel_id=1, source_target_pairs={{0,30},{2,0},{4,2},{6,4},{8,6},{10,8},{12,10},{14,12},{16,14},{18,... | collective-permute-start | bytes 49160 | tf_op jit(solution)/shard_map/ppermute | solution.py:43
  20.2 5.9 %collective-permute-start.2 = (bf16[2,32,128]{2,1,0:T(8,128)(2,1)S(1)}, bf16[2,32,128]{2,1,0:T(8,128)(2,1)S(1)}, u32[]{:S(2)}, u32[]{:S(2)}) collective-permute-start(bf16[2,32,128]{2,1,0:T(8,128)(2,1)S(1)} %collective-permute-done.1), channel_id=1, source_target_pairs={{0,2},{2,4},{4,6},{6,8},{8,10},{10,12},{12,14},{14,16},{16,18},{18... | collective-permute-start | bytes 49160 | tf_op jit(solution)/shard_map/ppermute | solution.py:41
  20.4 5.9 %collective-permute-start.9 = (bf16[2,32,128]{2,1,0:T(8,128)(2,1)S(1)}, bf16[2,32,128]{2,1,0:T(8,128)(2,1)S(1)}, u32[]{:S(2)}, u32[]{:S(2)}) collective-permute-start(bf16[2,32,128]{2,1,0:T(8,128)(2,1)S(1)} %collective-permute-done.8), channel_id=1, source_target_pairs={{0,30},{2,0},{4,2},{6,4},{8,6},{10,8},{12,10},{14,12},{16,14},{18,... | collective-permute-start | bytes 49160 | tf_op jit(solution)/shard_map/ppermute | solution.py:43
  26.1 5.9 %collective-permute-start.3 = (bf16[2,32,128]{2,1,0:T(8,128)(2,1)S(1)}, bf16[2,32,128]{2,1,0:T(8,128)(2,1)S(1)}, u32[]{:S(2)}, u32[]{:S(2)}) collective-permute-start(bf16[2,32,128]{2,1,0:T(8,128)(2,1)S(1)} %collective-permute-done.2), channel_id=1, source_target_pairs={{0,2},{2,4},{4,6},{6,8},{8,10},{10,12},{12,14},{14,16},{16,18},{18... | collective-permute-start | bytes 49160 | tf_op jit(solution)/shard_map/ppermute | solution.py:41
  26.3 5.9 %collective-permute-start.10 = (bf16[2,32,128]{2,1,0:T(8,128)(2,1)S(1)}, bf16[2,32,128]{2,1,0:T(8,128)(2,1)S(1)}, u32[]{:S(2)}, u32[]{:S(2)}) collective-permute-start(bf16[2,32,128]{2,1,0:T(8,128)(2,1)S(1)} %collective-permute-done.9), channel_id=1, source_target_pairs={{0,30},{2,0},{4,2},{6,4},{8,6},{10,8},{12,10},{14,12},{16,14},{18,... | collective-permute-start | bytes 49160 | tf_op jit(solution)/shard_map/ppermute | solution.py:43
  31.9 5.9 %collective-permute-start.4 = (bf16[2,32,128]{2,1,0:T(8,128)(2,1)S(1)}, bf16[2,32,128]{2,1,0:T(8,128)(2,1)S(1)}, u32[]{:S(2)}, u32[]{:S(2)}) collective-permute-start(bf16[2,32,128]{2,1,0:T(8,128)(2,1)S(1)} %collective-permute-done.3), channel_id=1, source_target_pairs={{0,2},{2,4},{4,6},{6,8},{8,10},{10,12},{12,14},{14,16},{16,18},{18... | collective-permute-start | bytes 49160 | tf_op jit(solution)/shard_map/ppermute | solution.py:41
  32.2 5.9 %collective-permute-start.11 = (bf16[2,32,128]{2,1,0:T(8,128)(2,1)S(1)}, bf16[2,32,128]{2,1,0:T(8,128)(2,1)S(1)}, u32[]{:S(2)}, u32[]{:S(2)}) collective-permute-start(bf16[2,32,128]{2,1,0:T(8,128)(2,1)S(1)} %collective-permute-done.10), channel_id=1, source_target_pairs={{0,30},{2,0},{4,2},{6,4},{8,6},{10,8},{12,10},{14,12},{16,14},{18,... | collective-permute-start | bytes 49160 | tf_op jit(solution)/shard_map/ppermute | solution.py:43
  37.8 5.9 %collective-permute-start.5 = (bf16[2,32,128]{2,1,0:T(8,128)(2,1)S(1)}, bf16[2,32,128]{2,1,0:T(8,128)(2,1)S(1)}, u32[]{:S(2)}, u32[]{:S(2)}) collective-permute-start(bf16[2,32,128]{2,1,0:T(8,128)(2,1)S(1)} %collective-permute-done.4), channel_id=1, source_target_pairs={{0,2},{2,4},{4,6},{6,8},{8,10},{10,12},{12,14},{14,16},{16,18},{18... | collective-permute-start | bytes 49160 | tf_op jit(solution)/shard_map/ppermute | solution.py:41
  38.0 5.9 %collective-permute-start.12 = (bf16[2,32,128]{2,1,0:T(8,128)(2,1)S(1)}, bf16[2,32,128]{2,1,0:T(8,128)(2,1)S(1)}, u32[]{:S(2)}, u32[]{:S(2)}) collective-permute-start(bf16[2,32,128]{2,1,0:T(8,128)(2,1)S(1)} %collective-permute-done.11), channel_id=1, source_target_pairs={{0,30},{2,0},{4,2},{6,4},{8,6},{10,8},{12,10},{14,12},{16,14},{18,... | collective-permute-start | bytes 49160 | tf_op jit(solution)/shard_map/ppermute | solution.py:43
  43.7 5.9 %collective-permute-start.6 = (bf16[2,32,128]{2,1,0:T(8,128)(2,1)S(1)}, bf16[2,32,128]{2,1,0:T(8,128)(2,1)S(1)}, u32[]{:S(2)}, u32[]{:S(2)}) collective-permute-start(bf16[2,32,128]{2,1,0:T(8,128)(2,1)S(1)} %collective-permute-done.5), channel_id=1, source_target_pairs={{0,2},{2,4},{4,6},{6,8},{8,10},{10,12},{12,14},{14,16},{16,18},{18... | collective-permute-start | bytes 49160 | tf_op jit(solution)/shard_map/ppermute | solution.py:41
  43.9 6.3 %collective-permute-start.13 = (bf16[2,32,128]{2,1,0:T(8,128)(2,1)S(1)}, bf16[2,32,128]{2,1,0:T(8,128)(2,1)S(1)}, u32[]{:S(2)}, u32[]{:S(2)}) collective-permute-start(bf16[2,32,128]{2,1,0:T(8,128)(2,1)S(1)} %collective-permute-done.12), channel_id=1, source_target_pairs={{0,30},{2,0},{4,2},{6,4},{8,6},{10,8},{12,10},{14,12},{16,14},{18,... | collective-permute-start | bytes 49160 | tf_op jit(solution)/shard_map/ppermute | solution.py:43
  49.5 5.9 %collective-permute-start.7 = (bf16[2,32,128]{2,1,0:T(8,128)(2,1)S(1)}, bf16[2,32,128]{2,1,0:T(8,128)(2,1)S(1)}, u32[]{:S(2)}, u32[]{:S(2)}) collective-permute-start(bf16[2,32,128]{2,1,0:T(8,128)(2,1)S(1)} %collective-permute-done.6), channel_id=1, source_target_pairs={{0,2},{2,4},{4,6},{6,8},{8,10},{10,12},{12,14},{14,16},{16,18},{18... | collective-permute-start | bytes 49160 | tf_op jit(solution)/shard_map/ppermute | solution.py:41
  50.2 6.1 %collective-permute-start.14 = (bf16[2,32,128]{2,1,0:T(8,128)(2,1)S(1)}, bf16[2,32,128]{2,1,0:T(8,128)(2,1)S(1)}, u32[]{:S(2)}, u32[]{:S(2)}) collective-permute-start(bf16[2,32,128]{2,1,0:T(8,128)(2,1)S(1)} %collective-permute-done.13), channel_id=1, source_target_pairs={{0,30},{2,0},{4,2},{6,4},{8,6},{10,8},{12,10},{14,12},{16,14},{18,... | collective-permute-start | bytes 49160 | tf_op jit(solution)/shard_map/ppermute | solution.py:43
  55.4 0.7 copy-start.2
  56.5 0.9 copy-start
  63.1 0.7 copy-start.3
  67.0 0.8 copy-start.1
Sparse Core Ops, SparseCore 0:
  67.9 56.5 reduce-scatter.1
